TPU v7x, 512 devices: a whole 4x4x16 slice. The times are simulated.
512 devices in a mesh: grp: 64 (over z, x_lo, core), rep: 8 (over y, x_hi).
Axes of the slice: x: 4 (x_hi: 2, x_lo: 2; x = x_hi * 2 + x_lo), y: 4, z: 16, core: 2. Of those that a mesh axis runs over, the one named last changes fastest.
Arguments:
- adjoint: bfloat16 [1024, 512], P('grp'), may hold values from -6 to 6
- active: int32 [1024, 512], P('grp'), may hold values 0 or 1
- counts: int32 [1024, 65536], P('rep', 'grp'), may hold values from 0 to 3, as said below
- src_degree: int32 [1024], P('rep'), may hold values from 8 to 256
- dst_degree: int32 [65536], P('grp'), may hold values from 8 to 256
- inputs: bfloat16 [65536, 512], P(('grp', 'rep')), may hold values from -6 to 6
- weight: bfloat16 [512, 512], replicated, may hold values from -0.25 to 0.25
Outputs:
- grad_input: bfloat16 [65536, 512], P(('grp', 'rep'))
- grad_weight: float32 [512, 512], P('rep')
Inputs may be any that keep to these rules, and one draw needn't show every extreme that they name: Edge counts; within an aligned tile of 16 source rows by 1024 destination columns the share of nonzero entries ranges from none to all, differing from tile to tile.
All inputs are finite; a program needn't handle non-finite values. No bound on the sum of `active` on one device may be relied on, other than what follows from the above.
Results may differ from a plain program's by a relative error of at most 0.0057.
Values may be sent and summed in bfloat16 or wider, within the bound.
A program may use at most 64 MiB of HBM per device.

v0:
```python
import jax
import jax.numpy as jnp
from jax import lax
from jax.sharding import PartitionSpec as P


def body(adjoint, active, counts, src_degree, dst_degree, inputs, weight):
    masked = (adjoint.astype(jnp.float32) * active.astype(jnp.float32)).astype(jnp.bfloat16)
    src_scale = lax.rsqrt(src_degree.astype(jnp.float32))
    dst_scale = lax.rsqrt(dst_degree.astype(jnp.float32))
    scaled = (counts.astype(jnp.float32) * src_scale[:, None] * dst_scale[None, :]).astype(
        jnp.bfloat16
    )
    my_scaled = lax.all_to_all(scaled, "rep", split_axis=1, concat_axis=0, tiled=True)
    all_masked = lax.all_gather(masked, "grp", axis=0, tiled=True)
    grad_pre = lax.dot_general(
        my_scaled, all_masked, (((0,), (0,)), ((), ())), preferred_element_type=jnp.float32
    )
    high = grad_pre.astype(jnp.bfloat16)
    low = (grad_pre - high.astype(jnp.float32)).astype(jnp.bfloat16)
    grad_input = lax.dot_general(
        high, weight, (((1,), (1,)), ((), ())), preferred_element_type=jnp.float32
    ).astype(jnp.bfloat16)
    vertex_total = inputs.shape[0] * lax.axis_size("grp") * lax.axis_size("rep")
    upper = lax.dot_general(
        inputs, high, (((0,), (0,)), ((), ())), preferred_element_type=jnp.float32
    )
    lower = lax.dot_general(
        inputs, low, (((0,), (0,)), ((), ())), preferred_element_type=jnp.float32
    )
    part = lax.psum_scatter(upper + lower, "rep", scatter_dimension=0, tiled=True)
    grad_weight = lax.psum(part, "grp")
    return (grad_input, grad_weight / vertex_total)


def solution(mesh):
    in_specs = (
        P("grp", None),
        P("grp", None),
        P("rep", "grp"),
        P("rep"),
        P("grp"),
        P(("grp", "rep"), None),
        P(),
    )
    out_specs = (P(("grp", "rep"), None), P("rep", None))
    return jax.shard_map(body, mesh=mesh, in_specs=in_specs, out_specs=out_specs, check_vma=False)
```

profile of v0, /device:TPU:1, one launch (start us, length us, event | category | flops | bytes accessed | tf_op | source)
XLA Modules:
  0.0 647.1 jit_solution(7749764605199366862)
XLA Ops:
  7.2 0.0 copy-start
  7.2 0.0 all-gather.2.cloned.1.call-start
  7.2 1.4 multiply_convert_fusion.1
  8.6 0.0 all-gather.2.cloned.1.call-update
  8.7 0.0 copy-start.3
  8.7 0.0 reduce-scatter.4.cloned.1.call-start
  8.7 0.0 copy-start.2
  8.7 1.2 copy.14
  10.0 0.0 copy-done.3
  10.0 0.0 copy-done.2
  10.0 0.2 multiply_convert_fusion
  10.2 15.2 %all_to_all.19 = bf16[128,8,128]{0,2,1:T(8,128)(2,1)S(1)} all-to-all(bf16[128,8,128]{0,2,1:T(8,128)(2,1)S(1)} %bitcast.13), channel_id=1, replica_groups=mesh['grp'=64,'rep'=8] {'rep'}, dimensions={1} | all-to-all | bytes 524288 | tf_op jit(solution)/shard_map/all_to_all | solution.py:14
  25.4 0.2 copy.15
  25.6 112.0 %all-gather.2.cloned.1.call-done = bf16[1024,512]{1,0:T(8,128)(2,1)} async-done(((bf16[16,512]{1,0:T(8,128)(2,1)}), bf16[1024,512]{1,0:T(8,128)(2,1)}) %all-gather.2.cloned.1.call-update) | async-done | bytes 1048592 | tf_op jit(solution)/shard_map/all_gather | solution.py:15
  137.6 0.0 copy-start.1
  137.6 1.6 fusion.5
  139.2 0.0 copy-done.1
  139.2 0.3 fusion.2
  139.5 0.3 fusion
  139.8 1.3 copy.17
  141.1 0.0 reduce-scatter.4.cloned.1.call-update
  141.2 0.0 all-reduce.2.cloned.1.call-start
  141.2 82.9 %reduce-scatter.4.cloned.1.call-done = f32[64,512]{1,0:T(8,128)} async-done(((f32[512,512]{1,0:T(8,128)}), f32[64,512]{1,0:T(8,128)}) %reduce-scatter.4.cloned.1.call-update) | async-done | bytes 131088
  224.1 1.7 copy.18
  225.8 0.0 all-reduce.2.cloned.1.call-update
  225.9 0.0 copy-done
  225.9 1.0 convolution_convert_fusion
  226.8 412.0 %all-reduce.2.cloned.1.call-done = f32[64,512]{0,1:T(8,128)} async-done(((f32[64,512]{0,1:T(8,128)}), f32[64,512]{0,1:T(8,128)}) %all-reduce.2.cloned.1.call-update) | async-done | bytes 131088 | tf_op jit(solution)/shard_map/psum | solution.py:32
  638.8 1.0 broadcast_multiply_fusion
  639.8 0.8 copy.16
  (2 shorter events, 0.0 us)
Async XLA Ops:
  7.2 218.7 %copy-start = (bf16[512,512]{1,0:T(8,128)(2,1)S(1)}, bf16[512,512]{1,0:T(8,128)(2,1)}, u32[]{:S(2)}) copy-start(bf16[512,512]{1,0:T(8,128)(2,1)} %param.13) | copy-start | bytes 1572868
  7.2 130.4 %all-gather.2.cloned.1.call-start = ((), (), s32[]{:S(2)}) async-start(), calls=%async_computation.2 | async-start | bytes 1064960 | tf_op jit(solution)/shard_map/all_gather | solution.py:15
  8.7 1.3 copy-start.3
  8.7 215.4 %reduce-scatter.4.cloned.1.call-start = ((), (), s32[]{:S(2)}) async-start(), calls=%async_computation.4 | async-start | bytes 1179648
  8.7 1.3 copy-start.2
  137.6 1.6 copy-start.1
  141.2 497.6 %all-reduce.2.cloned.1.call-start = ((), (), s32[]{:S(2)}) async-start(), calls=%async_computation.3 | async-start | bytes 524288 | tf_op jit(solution)/shard_map/psum | solution.py:32
Sparse Core Ops, SparseCore 0:
  10.7 126.8 all-gather.1
  142.0 82.0 reduce-scatter.3
  227.0 411.7 all-reduce.1
where the time goes:
time: 647 us
  waiting for transfers between devices  607 us (94%)
  blocking collectives  15.2 us (2%)
  between operations  13.9 us (2%)
    psum x1, waiting for transfers between devices, body(): grad_weight = lax.psum(part, 'grp')  412 us
    all_gather x1, waiting for transfers between devices, body(): all_masked = lax.all_gather(masked, 'grp', axis=0, tiled=True)  112 us
    unnamed x4, waiting for transfers between devices  82.9 us
    all_to_all x1, blocking collectives, body(): lax.all_to_all(scaled, 'rep', split_axis=1, concat_axis=0, tiled=True)  15.2 us
  transfers between devices with their start and end apart: 3, of which 3 were waited for; matrix products, arithmetic and copies ran while one was open for 0% of the time, Pallas kernels for 0%

commit v1 on v0

--- a/solution.py
+++ b/solution.py
@@ -12,7 +12,19 @@
         jnp.bfloat16
     )
     my_scaled = lax.all_to_all(scaled, "rep", split_axis=1, concat_axis=0, tiled=True)
-    all_masked = lax.all_gather(masked, "grp", axis=0, tiled=True)
+
+    def trace_the_array(u, device_axis):
+        return jnp.concatenate(
+            lax.all_to_all(
+                jnp.stack([u for _ in range(lax.axis_size(device_axis))]),
+                axis_name=device_axis,
+                split_axis=0,
+                concat_axis=0,
+            ),
+            0,
+        )
+
+    all_masked = trace_the_array(masked, "grp")
     grad_pre = lax.dot_general(
         my_scaled, all_masked, (((0,), (0,)), ((), ())), preferred_element_type=jnp.float32
     )

time: 647 us -> 600 us (0.927)
  waiting for transfers between devices: 607 us -> 548 us
  starting transfers between devices: 0.12 us -> 25.4 us
  blocking collectives: 15.2 us -> 0 us
    all_gather x1 -> x0, waiting for transfers between devices: 112 us -> none  [body(): all_masked = lax.all_gather(masked, 'grp', axis=0, tiled=True)]
    all_to_all x0 -> x2, waiting for transfers between devices: none -> 61.3 us  [the longest x1 53.7 us: trace_the_array(): lax.all_to_all(jnp.stack([u for _ in range(lax.axis_size(device_axis))]),...]
    all_to_all x0 -> x2, starting transfers between devices: none -> 25.3 us  [the longest x1 17.7 us: trace_the_array(): lax.all_to_all(jnp.stack([u for _ in range(lax.axis_size(device_axis))]),...]
    all_to_all x1 -> x0, blocking collectives: 15.2 us -> none  [body(): lax.all_to_all(scaled, 'rep', split_axis=1, concat_axis=0, tiled=True)]
    unnamed x4 -> x3, waiting for transfers between devices: 82.9 us -> 76 us
  transfers between devices with their start and end apart: 3 -> 4, of which waited for: 3 -> 4; matrix products, arithmetic and copies ran while one was open for 0% -> 0% of each run, Pallas kernels for 0% -> 0%
where the time goes in v1:
time: 600 us; the launch traced here: 599 us
  waiting for transfers between devices  548 us (91%)
  starting transfers between devices  25.4 us (4%)
  between operations  14.2 us (2%)
  local copies, waits for them, and re-layouts  7.64 us (1%)
    psum x1, waiting for transfers between devices, body(): grad_weight = lax.psum(part, 'grp')  411 us
    unnamed x3, waiting for transfers between devices  76 us
    all_to_all x1, waiting for transfers between devices, trace_the_array(): lax.all_to_all(jnp.stack([u for _ in range(lax.axis_size(device_axis))]),...  53.7 us
    all_to_all x1, starting transfers between devices, trace_the_array(): lax.all_to_all(jnp.stack([u for _ in range(lax.axis_size(device_axis))]),...  17.7 us
  transfers between devices with their start and end apart: 4, of which 4 were waited for; matrix products, arithmetic and copies ran while one was open for 0% of the time, Pallas kernels for 0%

profile of v1, /device:TPU:1, one launch (start us, length us, event | category | flops | bytes accessed | tf_op | source)
XLA Modules:
  0.0 599.5 jit_solution(16672947544697307248)
XLA Ops:
  7.2 0.0 copy-start
  7.2 0.0 copy-start.4
  7.2 1.3 copy.14
  8.5 0.0 copy-done.4
  8.5 0.0 copy-start.5
  8.5 0.6 copy-done.5
  9.2 0.9 multiply_convert_fusion
  10.1 0.0 copy-start.2
  10.1 0.0 copy-start.3
  10.1 7.6 %all-to-all-start = ((bf16[128,8,128]{0,2,1:T(8,128)(2,1)}), bf16[128,8,128]{0,2,1:T(8,128)(2,1)S(1)}, u32[]{:S(2)}, u32[]{:S(2)}) async-start(bf16[128,8,128]{0,2,1:T(8,128)(2,1)} %bitcast), calls=%async_computation | async-start | bytes 524288 | tf_op jit(solution)/shard_map/all_to_all | solution.py:14
  17.7 0.0 copy-done.2
  17.7 0.0 copy-done.3
  17.7 7.6 %all-to-all-done = bf16[128,8,128]{0,2,1:T(8,128)(2,1)S(1)} async-done(((bf16[128,8,128]{0,2,1:T(8,128)(2,1)}), bf16[128,8,128]{0,2,1:T(8,128)(2,1)S(1)}, u32[]{:S(2)}, u32[]{:S(2)}) %all-to-all-start) | async-done | bytes 262176 | tf_op jit(solution)/shard_map/all_to_all | solution.py:14
  25.4 1.1 stack.2
  26.5 17.7 %all-to-all-start.1 = ((bf16[64,16,512]{2,1,0:T(8,128)(2,1)}), bf16[64,16,512]{2,1,0:T(8,128)(2,1)S(1)}, u32[]{:S(2)}, u32[]{:S(2)}) async-start(bf16[64,16,512]{2,1,0:T(8,128)(2,1)} %stack.2), calls=%async_computation.1 | async-start | bytes 2097152 | tf_op jit(solution)/shard_map/all_to_all | solution.py:18
  44.2 0.0 reduce-scatter.4.cloned.1.call-start
  44.3 0.2 copy.15
  44.4 53.7 %all-to-all-done.1 = bf16[64,16,512]{2,1,0:T(8,128)(2,1)S(1)} async-done(((bf16[64,16,512]{2,1,0:T(8,128)(2,1)}), bf16[64,16,512]{2,1,0:T(8,128)(2,1)S(1)}, u32[]{:S(2)}, u32[]{:S(2)}) %all-to-all-start.1) | async-done | bytes 1048608 | tf_op jit(solution)/shard_map/all_to_all | solution.py:18
  98.1 0.0 copy-start.1
  98.1 0.3 fusion.5
  98.4 0.6 copy-done.1
  99.0 0.3 fusion.2
  99.3 0.3 fusion
  99.7 1.3 copy.17
  101.0 0.0 reduce-scatter.4.cloned.1.call-update
  101.0 0.0 all-reduce.2.cloned.1.call-start
  101.1 76.0 %reduce-scatter.4.cloned.1.call-done = f32[64,512]{1,0:T(8,128)} async-done(((f32[512,512]{1,0:T(8,128)}), f32[64,512]{1,0:T(8,128)}) %reduce-scatter.4.cloned.1.call-update) | async-done | bytes 131088
  177.1 1.7 copy.18
  178.8 0.0 all-reduce.2.cloned.1.call-update
  178.8 0.0 copy-done
  178.8 1.0 convolution_convert_fusion
  179.8 411.1 %all-reduce.2.cloned.1.call-done = f32[64,512]{0,1:T(8,128)} async-done(((f32[64,512]{0,1:T(8,128)}), f32[64,512]{0,1:T(8,128)}) %all-reduce.2.cloned.1.call-update) | async-done | bytes 131088 | tf_op jit(solution)/shard_map/psum | solution.py:44
  590.9 1.0 broadcast_multiply_fusion
  591.9 0.8 copy.16
  (3 shorter events, 0.0 us)
Async XLA Ops:
  7.2 171.7 %copy-start = (bf16[512,512]{1,0:T(8,128)(2,1)S(1)}, bf16[512,512]{1,0:T(8,128)(2,1)}, u32[]{:S(2)}) copy-start(bf16[512,512]{1,0:T(8,128)(2,1)} %param.13) | copy-start | bytes 1572868
  7.2 1.3 copy-start.4
  8.5 0.7 copy-start.5
  10.1 7.6 %copy-start.2 = (s32[16,512]{1,0:T(8,128)S(1)}, s32[16,512]{1,0:T(8,128)}, u32[]{:S(2)}) copy-start(s32[16,512]{1,0:T(8,128)} %param.8) | copy-start | bytes 98308
  10.1 7.6 %copy-start.3 = (bf16[16,512]{1,0:T(8,128)(2,1)S(1)}, bf16[16,512]{1,0:T(8,128)(2,1)}, u32[]{:S(2)}) copy-start(bf16[16,512]{1,0:T(8,128)(2,1)} %param.7) | copy-start | bytes 49156
  10.1 15.3 %all-to-all-start = ((bf16[128,8,128]{0,2,1:T(8,128)(2,1)}), bf16[128,8,128]{0,2,1:T(8,128)(2,1)S(1)}, u32[]{:S(2)}, u32[]{:S(2)}) async-start(bf16[128,8,128]{0,2,1:T(8,128)(2,1)} %bitcast), calls=%async_computation | async-start | bytes 524288 | tf_op jit(solution)/shard_map/all_to_all | solution.py:14
  26.5 71.6 %all-to-all-start.1 = ((bf16[64,16,512]{2,1,0:T(8,128)(2,1)}), bf16[64,16,512]{2,1,0:T(8,128)(2,1)S(1)}, u32[]{:S(2)}, u32[]{:S(2)}) async-start(bf16[64,16,512]{2,1,0:T(8,128)(2,1)} %stack.2), calls=%async_computation.1 | async-start | bytes 2097152 | tf_op jit(solution)/shard_map/all_to_all | solution.py:18
  44.2 132.8 %reduce-scatter.4.cloned.1.call-start = ((), (), s32[]{:S(2)}) async-start(), calls=%async_computation.4 | async-start | bytes 1179648
  98.1 0.9 copy-start.1
  101.0 489.9 %all-reduce.2.cloned.1.call-start = ((), (), s32[]{:S(2)}) async-start(), calls=%async_computation.3 | async-start | bytes 524288 | tf_op jit(solution)/shard_map/psum | solution.py:44
Sparse Core Ops, SparseCore 0:
  101.1 75.8 reduce-scatter.3
  180.0 410.8 all-reduce.1

commit v2 on v0

--- a/solution.py
+++ b/solution.py
@@ -2,6 +2,10 @@
 import jax.numpy as jnp
 from jax import lax
 from jax.sharding import PartitionSpec as P
+
+
+def _spread_roads(vals):
+    return jnp.sum(lax.all_gather(vals, "grp"), axis=0)
 
 
 def body(adjoint, active, counts, src_degree, dst_degree, inputs, weight):
@@ -29,7 +33,7 @@
         inputs, low, (((0,), (0,)), ((), ())), preferred_element_type=jnp.float32
     )
     part = lax.psum_scatter(upper + lower, "rep", scatter_dimension=0, tiled=True)
-    grad_weight = lax.psum(part, "grp")
+    grad_weight = _spread_roads(part)
     return (grad_input, grad_weight / vertex_total)
 
 

time: 647 us -> 368 us (0.57)
  waiting for transfers between devices: 607 us -> 323 us
    psum x1 -> x0, waiting for transfers between devices: 412 us -> none  [body(): grad_weight = lax.psum(part, 'grp')]
    all_gather x0 -> x1, waiting for transfers between devices: none -> 131 us  [_spread_roads(): return jnp.sum(lax.all_gather(vals, 'grp'), axis=0)]
    unnamed x4 -> x3, waiting for transfers between devices: 82.9 us -> 0.05 us
    reduce_scatter x0 -> x1, waiting for transfers between devices: none -> 82.1 us  [body(): lax.psum_scatter(upper + lower, 'rep', scatter_dimension=0, tiled=True)]
  transfers between devices with their start and end apart: 3 -> 3, of which waited for: 3 -> 3; matrix products, arithmetic and copies ran while one was open for 0% -> 1% of each run, Pallas kernels for 0% -> 0%
where the time goes in v2:
time: 368 us
  waiting for transfers between devices  323 us (88%)
  blocking collectives  15.2 us (4%)
  between operations  13.8 us (4%)
  other arithmetic  7.73 us (2%)
  matrix products  4.96 us (1%)
    all_gather x1, waiting for transfers between devices, _spread_roads(): return jnp.sum(lax.all_gather(vals, 'grp'), axis=0)  131 us
    all_gather x1, waiting for transfers between devices, body(): all_masked = lax.all_gather(masked, 'grp', axis=0, tiled=True)  111 us
    reduce_scatter x1, waiting for transfers between devices, body(): lax.psum_scatter(upper + lower, 'rep', scatter_dimension=0, tiled=True)  82.1 us
    all_to_all x1, blocking collectives, body(): lax.all_to_all(scaled, 'rep', split_axis=1, concat_axis=0, tiled=True)  15.2 us
  transfers between devices with their start and end apart: 3, of which 3 were waited for; matrix products, arithmetic and copies ran while one was open for 1% of the time, Pallas kernels for 0%

profile of v2, /device:TPU:1, one launch (start us, length us, event | category | flops | bytes accessed | tf_op | source)
XLA Modules:
  0.0 368.0 jit_solution(275225798145041987)
XLA Ops:
  7.2 0.0 copy-start
  7.2 0.0 all-gather.4.cloned.1.call-start
  7.2 1.4 multiply_convert_fusion.1
  8.6 0.0 all-gather.4.cloned.1.call-update
  8.7 0.0 reduce-scatter.4.cloned.1.call-start
  8.7 1.2 copy.13
  10.0 0.7 convert_rsqrt_fusion.1
  10.6 0.7 convert_rsqrt_fusion
  11.3 0.2 multiply_convert_fusion
  11.5 15.2 %all_to_all.19 = bf16[128,8,128]{0,2,1:T(8,128)(2,1)S(1)} all-to-all(bf16[128,8,128]{0,2,1:T(8,128)(2,1)S(1)} %bitcast.15), channel_id=1, replica_groups=mesh['grp'=64,'rep'=8] {'rep'}, dimensions={1} | all-to-all | bytes 524288 | tf_op jit(solution)/shard_map/all_to_all | solution.py:18
  26.7 0.2 copy.14
  26.9 110.7 %all-gather.4.cloned.1.call-done = bf16[1024,512]{1,0:T(8,128)(2,1)} async-done(((bf16[16,512]{1,0:T(8,128)(2,1)}), bf16[1024,512]{1,0:T(8,128)(2,1)}) %all-gather.4.cloned.1.call-update) | async-done | bytes 1048592 | tf_op jit(solution)/shard_map/all_gather | solution.py:19
  137.6 1.5 fusion.5
  139.1 1.2 fusion.2
  140.4 1.2 fusion
  141.6 1.3 copy.16
  142.9 0.0 reduce-scatter.4.cloned.1.call-update
  142.9 0.0 all-gather.6.cloned.1.call-start
  143.0 82.1 %reduce-scatter.4.cloned.1.call-done = f32[64,512]{1,0:T(8,128)} async-done(((f32[512,512]{1,0:T(8,128)}), f32[64,512]{1,0:T(8,128)}) %reduce-scatter.4.cloned.1.call-update) | async-done | bytes 131088 | tf_op jit(solution)/shard_map/reduce_scatter | solution.py:35
  225.1 0.0 all-gather.6.cloned.1.call-update
  225.1 0.0 copy-done
  225.1 1.0 convolution_convert_fusion
  226.1 130.6 %all-gather.6.cloned.1.call-done = f32[4096,512]{1,0:T(8,128)} async-done(((f32[64,512]{1,0:T(8,128)}), f32[4096,512]{1,0:T(8,128)}) %all-gather.6.cloned.1.call-update) | async-done | bytes 8388624 | tf_op jit(solution)/shard_map/all_gather | solution.py:8
  356.7 4.1 %reduce_sum.9 = f32[64,512]{1,0:T(8,128)S(1)} reduce(f32[64,64,512]{2,1,0:T(8,128)} %bitcast.12, f32[]{:T(128)} %constant.1.clone.1), dimensions={0}, to_apply=%region_1.0 | reduce | flops 2064384 | bytes 8519684 | tf_op jit(solution)/shard_map/reduce_sum | solution.py:8
  360.8 0.7 broadcast_multiply_fusion
Async XLA Ops:
  7.2 218.0 %copy-start = (bf16[512,512]{1,0:T(8,128)(2,1)S(1)}, bf16[512,512]{1,0:T(8,128)(2,1)}, u32[]{:S(2)}) copy-start(bf16[512,512]{1,0:T(8,128)(2,1)} %param.13) | copy-start | bytes 1572868
  7.2 130.4 %all-gather.4.cloned.1.call-start = ((), (), s32[]{:S(2)}) async-start(), calls=%async_computation.2 | async-start | bytes 1064960 | tf_op jit(solution)/shard_map/all_gather | solution.py:19
  8.7 216.4 %reduce-scatter.4.cloned.1.call-start = ((), (), s32[]{:S(2)}) async-start(), calls=%async_computation.4 | async-start | bytes 1179648 | tf_op jit(solution)/shard_map/reduce_scatter | solution.py:35
  142.9 213.8 %all-gather.6.cloned.1.call-start = ((), (), s32[]{:S(2)}) async-start(), calls=%async_computation.3 | async-start | bytes 8519680 | tf_op jit(solution)/shard_map/all_gather | solution.py:8
Sparse Core Ops, SparseCore 0:
  10.7 126.8 all-gather.3
  143.0 82.0 reduce-scatter.3
  227.3 129.4 all-gather.5
